TPU v7x, 32 devices: a whole 2x2x4 slice. The times are simulated.
32 devices in a mesh: groups: 2 (over x), loop: 16 (over z, y, core).
Axes of the slice: x: 2, y: 2, z: 4, core: 2. Of those that a mesh axis runs over, the one named last changes fastest.
Arguments:
- queries: bfloat16 [256, 4, 64, 128], P(('groups', 'loop')), parts along dimension 0, may hold values from -16 to 16
- new_keys: bfloat16 [256, 4, 4, 128], P(('groups', 'loop')), parts along dimension 0, may hold values from -8 to 8
- new_values: bfloat16 [256, 4, 4, 128], P(('groups', 'loop')), parts along dimension 0, may hold values from -12 to 12
- suffix_keys: bfloat16 [256, 256, 4, 128], P(('groups', 'loop')), parts along dimension 0, may hold values from -8 to 8
- suffix_values: bfloat16 [256, 256, 4, 128], P(('groups', 'loop')), parts along dimension 0, may hold values from -12 to 12
- suffix_len: int32 [256], P(('groups', 'loop')), parts along dimension 0, may hold values from 1 to 256, 16384 in all
- prefix_keys: bfloat16 [32, 64, 4, 128], P(('groups', 'loop')), parts along dimension 0, may hold values from -8 to 8
- prefix_values: bfloat16 [32, 64, 4, 128], P(('groups', 'loop')), parts along dimension 0, may hold values from -12 to 12
- block_ids: int32 [32], P(('groups', 'loop')), parts along dimension 0, may hold values from 0 to 15, each once
- block_lists: int32 [256, 4], P(('groups', 'loop')), parts along dimension 0, may hold values from 0 to 15, all different within a row
Outputs:
- attended: bfloat16 [256, 4, 64, 128], P(('groups', 'loop')), parts along dimension 0
There are 2 independent parts, one for each index of `groups`. A program takes and returns all parts, laid end to end along the dimension named above; each array names one. Nothing has to cross between parts.
Inputs may be any that keep to these rules, and one draw needn't show every extreme that they name: `block_ids`: each slot holds a different block. `block_lists`: each request names 4 different blocks; every block is named by some request. `suffix_len`: some request uses all 256 slots.
All inputs are finite; a program needn't handle non-finite values. No bound on the sum of `suffix_len` on one device may be relied on, other than what follows from the above.
Results may differ from a plain program's by a relative error of at most 0.004.
Values may be sent and summed in bfloat16 or wider, within the bound.
No kernel may reach another device: no remote copies, remote signals or barrier semaphores. Data moves between devices by JAX's collectives and lax.ppermute only.
A program may use at most 64 MiB of HBM per device.

v0:
```python
import math
import jax
import jax.numpy as jnp
from jax import lax
from jax.sharding import PartitionSpec as P


def per_device(
    queries,
    new_keys,
    new_values,
    suffix_keys,
    suffix_values,
    suffix_len,
    prefix_keys,
    prefix_values,
    block_ids,
    block_lists,
):
    requests, decode_steps, head_count, head_width = queries.shape
    key_heads = new_keys.shape[2]
    group_size = head_count // key_heads
    score_scale = 1.0 / math.sqrt(head_width)
    per_request = decode_steps * group_size
    grouped = queries.reshape(requests, decode_steps, key_heads, group_size, head_width)
    grouped = grouped.transpose(0, 2, 1, 3, 4).reshape(requests, key_heads, per_request, head_width)
    suffix_scores = (
        jnp.einsum("rgmd,rkgd->rgmk", grouped, suffix_keys, preferred_element_type=jnp.float32)
        * score_scale
    )
    suffix_slots = suffix_keys.shape[1]
    suffix_shown = (jnp.arange(suffix_slots)[None, :] < suffix_len[:, None])[:, None, None, :]
    fresh_scores = (
        jnp.einsum("rgmd,rtgd->rgmt", grouped, new_keys, preferred_element_type=jnp.float32)
        * score_scale
    )
    step_of_row = jnp.arange(per_request) // group_size
    fresh_shown = (jnp.arange(decode_steps)[None, :] <= step_of_row[:, None])[None, None]
    local_top = jnp.maximum(
        jnp.max(jnp.where(suffix_shown, suffix_scores, -jnp.inf), axis=-1),
        jnp.max(jnp.where(fresh_shown, fresh_scores, -jnp.inf), axis=-1),
    )
    gathered = (
        lax.all_gather(prefix_keys, "loop", axis=0, tiled=True),
        lax.all_gather(prefix_values, "loop", axis=0, tiled=True),
        lax.all_gather(block_ids, "loop", axis=0, tiled=True),
    )
    all_keys, all_values, all_ids = gathered
    block_count = all_ids.shape[0]
    named_count = block_lists.shape[1]
    block_size = all_keys.shape[1]
    matches = all_ids[None, None, :] == block_lists[:, :, None]
    slots = jnp.sum(
        jnp.where(matches, jnp.arange(block_count, dtype=jnp.int32)[None, None, :], 0), axis=2
    )
    prior_keys = all_keys[slots].reshape(requests, named_count * block_size, key_heads, head_width)
    prior_values = all_values[slots].reshape(
        requests, named_count * block_size, key_heads, head_width
    )
    prior_scores = (
        jnp.einsum("rgmd,rkgd->rgmk", grouped, prior_keys, preferred_element_type=jnp.float32)
        * score_scale
    )
    whole_top = jnp.maximum(local_top, jnp.max(prior_scores, axis=-1))
    suffix_weights = jnp.where(suffix_shown, jnp.exp(suffix_scores - whole_top[..., None]), 0.0)
    fresh_weights = jnp.where(fresh_shown, jnp.exp(fresh_scores - whole_top[..., None]), 0.0)
    sums = jnp.sum(suffix_weights, axis=-1) + jnp.sum(fresh_weights, axis=-1)
    weighted = jnp.einsum(
        "rgmk,rkgd->rgmd",
        suffix_weights.astype(jnp.bfloat16),
        suffix_values,
        preferred_element_type=jnp.float32,
    )
    weighted = weighted + jnp.einsum(
        "rgmt,rtgd->rgmd",
        fresh_weights.astype(jnp.bfloat16),
        new_values,
        preferred_element_type=jnp.float32,
    )
    sums, weighted = (sums, weighted)
    prior_weights = jnp.exp(prior_scores - whole_top[..., None])
    sums = sums + jnp.sum(prior_weights, axis=-1)
    weighted = weighted + jnp.einsum(
        "rgmk,rkgd->rgmd",
        prior_weights.astype(jnp.bfloat16),
        prior_values,
        preferred_element_type=jnp.float32,
    )
    mixed = weighted / sums[..., None]
    mixed = mixed.reshape(requests, key_heads, decode_steps, group_size, head_width).transpose(
        0, 2, 1, 3, 4
    )
    return mixed.reshape(requests, decode_steps, head_count, head_width).astype(jnp.bfloat16)


def solution(mesh):
    in_specs = (
        P(("groups", "loop"), None, None, None),
        P(("groups", "loop"), None, None, None),
        P(("groups", "loop"), None, None, None),
        P(("groups", "loop"), None, None, None),
        P(("groups", "loop"), None, None, None),
        P(("groups", "loop")),
        P(("groups", "loop"), None, None, None),
        P(("groups", "loop"), None, None, None),
        P(("groups", "loop")),
        P(("groups", "loop"), None),
    )
    out_specs = P(("groups", "loop"), None, None, None)
    return jax.shard_map(
        per_device, mesh=mesh, in_specs=in_specs, out_specs=out_specs, check_vma=False
    )
```

profile of v0, /device:TPU:0, one launch (start us, length us, event | category | flops | bytes accessed | tf_op | source)
XLA Modules:
  0.0 106.5 jit_solution(6860243202798953930)
XLA Ops:
  6.5 0.0 copy-start
  6.5 0.0 all-gather.3.cloned.1.call-start
  6.5 1.6 %copy.70 = bf16[1,64,4,128]{3,1,2,0:T(8,128)(2,1)} copy(bf16[1,64,4,128]{3,2,1,0:T(4,128)(2,1)} %param.16) | data formatting | bytes 131072 | tf_op args[6]
  8.2 0.0 all-gather.3.cloned.1.call-update
  8.2 0.0 all-gather.5.cloned.1.call-start
  8.2 1.5 %copy.76 = bf16[1,64,4,128]{3,1,2,0:T(8,128)(2,1)} copy(bf16[1,64,4,128]{3,2,1,0:T(4,128)(2,1)} %param.17) | data formatting | bytes 131072 | tf_op args[7]
  9.7 0.0 all-gather.5.cloned.1.call-update
  10.4 1.3 %dynamic-slice = u32[1]{0:T(128)} dynamic-slice(u32[32]{0:T(128)} %constant.41, u32[]{:T(128)S(6)} %add.41), dynamic_slice_sizes={1} | dynamic-slice | bytes 12
  11.7 0.7 dynamic-update-slice
  12.4 1.1 %copy.67 = bf16[8,4,4,16,128]{4,3,2,1,0:T(8,128)(2,1)S(1)} copy(bf16[8,4,4,16,128]{4,3,1,2,0:T(8,128)(2,1)} %bitcast.41) | data formatting | bytes 1048576 | tf_op jit(solution)/shard_map/transpose | solution.py:26
  13.5 13.8 %all-reduce = s32[16]{0:T(128)S(1)} all-reduce(s32[16]{0:T(128)S(1)} %dynamic-update-slice), channel_id=1, replica_groups=mesh['groups'=2,'loop'=16] {'loop'}, use_global_device_ids=true, to_apply=%add | all-reduce | flops 16 | bytes 128
  27.3 0.9 select_reduce_fusion.2
  28.2 0.1 copy.71
  28.3 0.1 reshape.102
  28.4 0.7 iota_compare_fusion
  29.1 1.2 %select_reduce_fusion.1 = (f32[8,4,64]{2,1,0:T(4,128)S(1)}, f32[8,4,64,4]{2,3,1,0:T(4,128)S(1)}) fusion(pred[64,4]{0,1:T(4,128)(4,1)S(1)} %iota_compare_fusion.1, bf16[8,4,64,128]{3,2,1,0:T(8,128)(2,1)S(1)} %bitcast.37, bf16[8,4,4,128]{3,2,1,0:T(4,128)(2,1)} %param.11), kind=kOutput, calls=%fused_computation.31 | convolution fusion | flops 2119680 | bytes 598272 | tf_op jit(solution)/shard_map/rgmd,rtgd->rgmt/dot_general | solution.py:34
  30.3 0.0 copy-done
  30.3 2.2 %select_reduce_fusion = (f32[8,4,64]{2,1,0:T(4,128)S(1)}, f32[8,4,64,256]{3,2,1,0:T(8,128)}) fusion(pred[8,256]{1,0:T(8,128)(4,1)S(1)} %iota_compare_fusion, bf16[8,4,64,128]{3,2,1,0:T(8,128)(2,1)S(1)} %bitcast.38, bf16[8,256,4,128]{3,2,1,0:T(4,128)(2,1)S(1)} %copy-done), kind=kOutput, calls=%fused_computation.14 | convolution fusion | flops 135788544 | bytes 4728832 | tf_op jit(solution)/shard_map/rgmd,rkgd->rgmk/dot_general | solution.py:28
  32.5 17.6 %all-gather.3.cloned.1.call-done = bf16[16,64,4,128]{3,1,2,0:T(8,128)(2,1)} async-done(((bf16[1,64,4,128]{3,1,2,0:T(8,128)(2,1)}), bf16[16,64,4,128]{3,1,2,0:T(8,128)(2,1)}) %all-gather.3.cloned.1.call-update) | async-done | bytes 1048592 | tf_op jit(solution)/shard_map/all_gather | solution.py:44
  50.1 3.3 %gather_fusion = bf16[32,64,4,128]{3,1,2,0:T(8,128)(2,1)} fusion(bf16[16,64,4,128]{3,1,2,0:T(8,128)(2,1)} %all-gather.3.cloned.1.call-done, s32[1024]{0:T(1024)S(1)} %pad_clamp_fusion), kind=kCustom, calls=%fused_computation | custom fusion | bytes 4194432 | tf_op jit(solution)/shard_map/gather | solution.py:56
  53.5 1.8 %copy.72 = bf16[32,64,4,128]{3,1,0,2:T(8,128)(2,1)S(1)} copy(bf16[32,64,4,128]{3,1,2,0:T(8,128)(2,1)} %gather_fusion) | data formatting | bytes 4194304 | tf_op jit(solution)/shard_map/gather | solution.py:56
  55.2 0.0 copy-start.4
  55.2 2.2 %bitcast_reduce_fusion = (f32[8,4,64]{2,1,0:T(4,128)S(1)}, f32[8,4,256,64]{2,3,1,0:T(8,128)}) fusion(bf16[8,4,64,128]{3,2,1,0:T(8,128)(2,1)S(1)} %bitcast.39, bf16[8,256,4,128]{3,1,0,2:T(8,128)(2,1)S(1)} %bitcast.36), kind=kOutput, calls=%fused_computation.3 | convolution fusion | flops 135264256 | bytes 4726784 | tf_op jit(solution)/shard_map/rgmd,rkgd->rgmk/dot_general | solution.py:61
  57.4 0.1 fusion.33
  57.5 0.0 copy-done.4
  57.5 0.4 fusion.35
  57.8 31.3 %all-gather.5.cloned.1.call-done = bf16[16,64,4,128]{3,1,2,0:T(8,128)(2,1)} async-done(((bf16[1,64,4,128]{3,1,2,0:T(8,128)(2,1)}), bf16[16,64,4,128]{3,1,2,0:T(8,128)(2,1)}) %all-gather.5.cloned.1.call-update) | async-done | bytes 1048592 | tf_op jit(solution)/shard_map/all_gather | solution.py:45
  89.2 3.4 %gather_fusion.1 = bf16[32,64,4,128]{3,1,2,0:T(8,128)(2,1)} fusion(bf16[16,64,4,128]{3,1,2,0:T(8,128)(2,1)} %all-gather.5.cloned.1.call-done, s32[1024]{0:T(1024)S(1)} %pad_clamp_fusion), kind=kCustom, calls=%fused_computation.1 | custom fusion | bytes 4194432 | tf_op jit(solution)/shard_map/gather | solution.py:57
  92.5 0.0 copy-start.1
  92.5 0.0 copy-start.2
  92.5 1.9 %copy.77 = bf16[32,64,4,128]{3,1,0,2:T(8,128)(2,1)S(1)} copy(bf16[32,64,4,128]{3,1,2,0:T(8,128)(2,1)} %gather_fusion.1) | data formatting | bytes 4194304 | tf_op jit(solution)/shard_map/gather | solution.py:57
  94.5 0.3 copy-done.1
  94.7 0.6 copy-done.2
  95.4 0.0 copy-start.3
  95.4 1.6 %fusion.11 = (f32[8,4,64]{2,1,0:T(4,128)S(1)}, f32[8,4,64]{2,1,0:T(4,128)S(1)}) fusion(f32[8,4,64,256]{3,2,1,0:T(8,128)S(1)} %copy-done.1, f32[8,4,64]{2,1,0:T(4,128)S(1)} %bitcast.45, pred[8,256]{1,0:T(8,128)(4,1)S(1)} %iota_compare_fusion, f32[8,4,256,64]{2,3,1,0:T(8,128)S(1)} %copy-done.2), kind=kLoop, calls=%fused_computation.17 | loop fusion | flops 3665920 | bytes 4220928 | tf_op jit(solution)/shard_map/reduce_sum | solution.py:67
  97.0 0.0 copy-done.3
  97.0 0.9 fusion.13
  97.9 0.9 fusion.22
  98.8 0.9 copy.79
  (7 shorter events, 0.0 us)
Async XLA Ops:
  6.5 23.7 %copy-start = (bf16[8,256,4,128]{3,2,1,0:T(4,128)(2,1)S(1)}, bf16[8,256,4,128]{3,2,1,0:T(4,128)(2,1)}, u32[]{:S(2)}) copy-start(bf16[8,256,4,128]{3,2,1,0:T(4,128)(2,1)} %param.13) | copy-start | bytes 6291460
  6.5 43.6 %all-gather.3.cloned.1.call-start = ((), (), s32[]{:S(2)}) async-start(), calls=%async_computation | async-start | bytes 1114112 | tf_op jit(solution)/shard_map/all_gather | solution.py:44
  8.2 81.0 %all-gather.5.cloned.1.call-start = ((), (), s32[]{:S(2)}) async-start(), calls=%async_computation.1 | async-start | bytes 1114112 | tf_op jit(solution)/shard_map/all_gather | solution.py:45
  55.2 2.3 %copy-start.4 = (bf16[8,4,4,128]{3,2,1,0:T(4,128)(2,1)S(1)}, bf16[8,4,4,128]{3,2,1,0:T(4,128)(2,1)}, u32[]{:S(2)}) copy-start(bf16[8,4,4,128]{3,2,1,0:T(4,128)(2,1)} %param.12) | copy-start | bytes 98308
  92.5 2.2 %copy-start.1 = (f32[8,4,64,256]{3,2,1,0:T(8,128)S(1)}, f32[8,4,64,256]{3,2,1,0:T(8,128)}, u32[]{:S(2)}) copy-start(f32[8,4,64,256]{3,2,1,0:T(8,128)} %get-tuple-element.10) | copy-start | bytes 6291460
  92.5 2.9 %copy-start.2 = (f32[8,4,256,64]{2,3,1,0:T(8,128)S(1)}, f32[8,4,256,64]{2,3,1,0:T(8,128)}, u32[]{:S(2)}) copy-start(f32[8,4,256,64]{2,3,1,0:T(8,128)} %get-tuple-element.8) | copy-start | bytes 6291460
  95.4 1.6 %copy-start.3 = (bf16[8,256,4,128]{3,2,1,0:T(4,128)(2,1)S(1)}, bf16[8,256,4,128]{3,2,1,0:T(4,128)(2,1)}, u32[]{:S(2)}) copy-start(bf16[8,256,4,128]{3,2,1,0:T(4,128)(2,1)} %param.14) | copy-start | bytes 6291460
Sparse Core Ops, SparseCore 0:
  9.5 40.5 all-gather.2
  52.3 36.8 all-gather.4
where the time goes:
time: 107 us
  waiting for transfers between devices  49 us (46%)
  local copies, waits for them, and re-layouts  18.5 us (17%)
  between operations  14.2 us (13%)
  blocking collectives  13.8 us (13%)
  matrix products  7.74 us (7%)
  other arithmetic  3.32 us (3%)
    all_gather x1, waiting for transfers between devices, per_device(): lax.all_gather(prefix_values, 'loop', axis=0, tiled=True)  31.3 us
    all_gather x1, waiting for transfers between devices, per_device(): lax.all_gather(prefix_keys, 'loop', axis=0, tiled=True)  17.6 us
    unnamed x1, blocking collectives  13.8 us
    unnamed x15, local copies, waits for them, and re-layouts  6.01 us
    gather x2, local copies, waits for them, and re-layouts, per_device(): all_values[slots]  5.31 us
    gather x2, local copies, waits for them, and re-layouts, per_device(): all_keys[slots]  5.09 us
    dot_general x1, matrix products, per_device(): jnp.einsum('rgmd,rkgd->rgmk', grouped, suffix_keys, preferred_element_typ...  2.22 us
    dot_general x1, matrix products, per_device(): jnp.einsum('rgmd,rkgd->rgmk', grouped, prior_keys, preferred_element_type...  2.16 us
  transfers between devices with their start and end apart: 2, of which 2 were waited for; matrix products, arithmetic and copies ran while one was open for 16% of the time, Pallas kernels for 0%

commit v1 on v0

--- a/solution.py
+++ b/solution.py
@@ -3,6 +3,22 @@
 import jax.numpy as jnp
 from jax import lax
 from jax.sharding import PartitionSpec as P
+
+
+def gather_around(x, axis, dim):
+    ways, here, hop = (lax.axis_size(axis), lax.axis_index(axis), x.shape[dim])
+    shape = [n * ways if d == dim else n for d, n in enumerate(x.shape)]
+    full = lax.dynamic_update_slice_in_dim(jnp.zeros(shape, x.dtype), x, here * hop, axis=dim)
+    going_up = going_down = x
+    for far in range(1, ways // 2 + 1):
+        going_up = lax.ppermute(going_up, axis, [(d, (d + 1) % ways) for d in range(ways)])
+        full = lax.dynamic_update_slice_in_dim(full, going_up, (here - far) % ways * hop, axis=dim)
+        if 2 * far < ways:
+            going_down = lax.ppermute(going_down, axis, [(d, (d - 1) % ways) for d in range(ways)])
+            full = lax.dynamic_update_slice_in_dim(
+                full, going_down, (here + far) % ways * hop, axis=dim
+            )
+    return full
 
 
 def per_device(
@@ -42,7 +58,7 @@
     )
     gathered = (
         lax.all_gather(prefix_keys, "loop", axis=0, tiled=True),
-        lax.all_gather(prefix_values, "loop", axis=0, tiled=True),
+        gather_around(prefix_values, "loop", 0),
         lax.all_gather(block_ids, "loop", axis=0, tiled=True),
     )
     all_keys, all_values, all_ids = gathered

time: 107 us -> 105 us (0.981)
  starting transfers between devices: 0.04 us -> 32.6 us
  waiting for transfers between devices: 49 us -> 18.2 us
  blocking collectives: 13.8 us -> 10.2 us
    ppermute x0 -> x15, starting transfers between devices: none -> 32.6 us  [the longest x7 32 us: gather_around(): lax.ppermute(going_down, axis, [(d, (d - 1) % ways) for d in range(ways)])]
    all_gather x1 -> x0, waiting for transfers between devices: 31.3 us -> none  [per_device(): lax.all_gather(prefix_values, 'loop', axis=0, tiled=True)]
    ppermute x0 -> x15, waiting for transfers between devices: none -> 18.2 us  [the longest x8 18.1 us: gather_around(): lax.ppermute(going_up, axis, [(d, (d + 1) % ways) for d in range(ways)])]
    all_gather x1, waiting for transfers between devices: 17.6 us -> 0.01 us  [per_device(): lax.all_gather(prefix_keys, 'loop', axis=0, tiled=True)]
    unnamed x1, blocking collectives: 13.8 us -> 10.2 us
    dot_general x1, matrix products: 2.16 us -> 0.95 us  [per_device(): jnp.einsum('rgmd,rkgd->rgmk', grouped, prior_keys, preferred_element_type...]
    dot_general x1, matrix products: 2.22 us -> 3.32 us  [per_device(): jnp.einsum('rgmd,rkgd->rgmk', grouped, suffix_keys, preferred_element_typ...]
    unnamed x15 -> x21, local copies, waits for them, and re-layouts: 6.01 us -> 5.32 us
  transfers between devices with their start and end apart: 2 -> 16, of which waited for: 2 -> 8; matrix products, arithmetic and copies ran while one was open for 16% -> 16% of each run, Pallas kernels for 0% -> 0%
where the time goes in v1:
time: 105 us
  starting transfers between devices  32.6 us (31%)
  local copies, waits for them, and re-layouts  19.2 us (18%)
  waiting for transfers between devices  18.2 us (17%)
  between operations  14.5 us (14%)
  blocking collectives  10.2 us (10%)
  matrix products  6.85 us (7%)
  other arithmetic  3.31 us (3%)
    ppermute x7, starting transfers between devices, gather_around(): lax.ppermute(going_down, axis, [(d, (d - 1) % ways) for d in range(ways)])  32 us
    ppermute x8, waiting for transfers between devices, gather_around(): lax.ppermute(going_up, axis, [(d, (d + 1) % ways) for d in range(ways)])  18.1 us
    unnamed x1, blocking collectives  10.2 us
    unnamed x21, local copies, waits for them, and re-layouts  5.32 us
    gather x2, local copies, waits for them, and re-layouts, per_device(): all_values[slots]  5.27 us
    gather x2, local copies, waits for them, and re-layouts, per_device(): all_keys[slots]  5.21 us
    dot_general x1, matrix products, per_device(): jnp.einsum('rgmd,rkgd->rgmk', grouped, suffix_keys, preferred_element_typ...  3.32 us
  transfers between devices with their start and end apart: 16, of which 8 were waited for; matrix products, arithmetic and copies ran while one was open for 16% of the time, Pallas kernels for 0%

profile of v1, /device:TPU:0, one launch (start us, length us, event | category | flops | bytes accessed | tf_op | source)
XLA Modules:
  0.0 104.9 jit_solution(13549708355018907389)
XLA Ops:
  6.5 0.0 copy-start
  6.5 0.0 all-gather.2.cloned.1.call-start
  6.5 0.2 broadcast_in_dim.76
  6.8 1.0 fusion.46
  7.8 0.5 collective-permute-start
  8.3 5.0 %collective-permute-start.1 = (bf16[1,64,4,128]{3,1,2,0:T(8,128)(2,1)S(1)}, bf16[1,64,4,128]{3,1,2,0:T(8,128)(2,1)S(1)}, u32[]{:S(2)}, u32[]{:S(2)}) collective-permute-start(bf16[1,64,4,128]{3,1,2,0:T(8,128)(2,1)S(1)} %get-tuple-element.7), channel_id=1, source_target_pairs={{0,15},{1,0},{2,1},{3,2},{4,3},{5,4},{6,5},{7,6},{8,7},{9,8},{10,9... | collective-permute-start | bytes 196616 | tf_op jit(solution)/shard_map/ppermute | solution.py:17
  13.4 1.5 %copy.92 = bf16[1,64,4,128]{3,1,2,0:T(8,128)(2,1)} copy(bf16[1,64,4,128]{3,2,1,0:T(4,128)(2,1)} %param.16) | data formatting | bytes 131072 | tf_op args[6]
  14.9 0.0 all-gather.2.cloned.1.call-update
  15.8 1.2 %dynamic-slice = u32[1]{0:T(128)} dynamic-slice(u32[32]{0:T(128)} %constant.140, u32[]{:T(128)S(6)} %add.202), dynamic_slice_sizes={1} | dynamic-slice | bytes 12
  17.0 0.8 dynamic-update-slice
  17.8 10.2 %all-reduce = s32[16]{0:T(128)S(1)} all-reduce(s32[16]{0:T(128)S(1)} %dynamic-update-slice), channel_id=1, replica_groups=mesh['groups'=2,'loop'=16] {'loop'}, use_global_device_ids=true, to_apply=%add | all-reduce | flops 16 | bytes 128
  28.0 0.9 select_reduce_fusion.2
  28.9 0.7 iota_compare_fusion
  29.6 0.1 copy.93
  29.7 0.1 reshape.102
  29.8 1.9 %copy.89 = bf16[8,4,4,16,128]{4,3,2,1,0:T(8,128)(2,1)} copy(bf16[8,4,4,16,128]{4,3,1,2,0:T(8,128)(2,1)} %bitcast.41) | data formatting | bytes 1048576 | tf_op jit(solution)/shard_map/transpose | solution.py:42
  31.7 0.0 copy-done
  31.7 3.3 %select_reduce_fusion = (f32[8,4,64]{2,1,0:T(4,128)S(1)}, f32[8,4,64,256]{3,2,1,0:T(8,128)}) fusion(pred[8,256]{1,0:T(8,128)(4,1)S(1)} %iota_compare_fusion, bf16[8,4,64,128]{3,2,1,0:T(8,128)(2,1)} %bitcast.37, bf16[8,256,4,128]{3,2,1,0:T(4,128)(2,1)S(1)} %copy-done), kind=kOutput, calls=%fused_computation.14 | convolution fusion | flops 135788544 | bytes 4728832 | tf_op jit(solution)/shard_map/rgmd,rkgd->rgmk/dot_general | solution.py:44
  35.0 0.0 copy-done.2
  35.0 0.0 copy-done.7
  35.0 0.4 select_reduce_fusion.1
  35.5 0.0 collective-permute-done
  35.5 0.1 collective-permute-start.2
  35.5 0.0 collective-permute-done.1
  35.5 4.4 %collective-permute-start.3 = (bf16[1,64,4,128]{3,1,2,0:T(8,128)(2,1)S(1)}, bf16[1,64,4,128]{3,1,2,0:T(8,128)(2,1)S(1)}, u32[]{:S(2)}, u32[]{:S(2)}) collective-permute-start(bf16[1,64,4,128]{3,1,2,0:T(8,128)(2,1)S(1)} %collective-permute-done.1), channel_id=1, source_target_pairs={{0,15},{1,0},{2,1},{3,2},{4,3},{5,4},{6,5},{7,6},{8,7},{9,8},{10,9... | collective-permute-start | bytes 196616 | tf_op jit(solution)/shard_map/ppermute | solution.py:17
  40.0 2.0 %collective-permute-done.2 = bf16[1,64,4,128]{3,1,2,0:T(8,128)(2,1)S(1)} collective-permute-done((bf16[1,64,4,128]{3,1,2,0:T(8,128)(2,1)S(1)}, bf16[1,64,4,128]{3,1,2,0:T(8,128)(2,1)S(1)}, u32[]{:S(2)}, u32[]{:S(2)}) %collective-permute-start.2) | collective-permute-done | bytes 65568 | tf_op jit(solution)/shard_map/ppermute | solution.py:14
  42.0 0.0 collective-permute-start.4
  42.0 0.1 collective-permute-done.3
  42.1 4.6 %collective-permute-start.5 = (bf16[1,64,4,128]{3,1,2,0:T(8,128)(2,1)S(1)}, bf16[1,64,4,128]{3,1,2,0:T(8,128)(2,1)S(1)}, u32[]{:S(2)}, u32[]{:S(2)}) collective-permute-start(bf16[1,64,4,128]{3,1,2,0:T(8,128)(2,1)S(1)} %collective-permute-done.3), channel_id=1, source_target_pairs={{0,15},{1,0},{2,1},{3,2},{4,3},{5,4},{6,5},{7,6},{8,7},{9,8},{10,9... | collective-permute-start | bytes 196616 | tf_op jit(solution)/shard_map/ppermute | solution.py:17
  46.7 2.3 %collective-permute-done.4 = bf16[1,64,4,128]{3,1,2,0:T(8,128)(2,1)S(1)} collective-permute-done((bf16[1,64,4,128]{3,1,2,0:T(8,128)(2,1)S(1)}, bf16[1,64,4,128]{3,1,2,0:T(8,128)(2,1)S(1)}, u32[]{:S(2)}, u32[]{:S(2)}) %collective-permute-start.4) | collective-permute-done | bytes 65568 | tf_op jit(solution)/shard_map/ppermute | solution.py:14
  49.0 0.0 collective-permute-start.6
  49.0 0.0 collective-permute-done.5
  49.0 4.4 %collective-permute-start.7 = (bf16[1,64,4,128]{3,1,2,0:T(8,128)(2,1)S(1)}, bf16[1,64,4,128]{3,1,2,0:T(8,128)(2,1)S(1)}, u32[]{:S(2)}, u32[]{:S(2)}) collective-permute-start(bf16[1,64,4,128]{3,1,2,0:T(8,128)(2,1)S(1)} %collective-permute-done.5), channel_id=1, source_target_pairs={{0,15},{1,0},{2,1},{3,2},{4,3},{5,4},{6,5},{7,6},{8,7},{9,8},{10,9... | collective-permute-start | bytes 196616 | tf_op jit(solution)/shard_map/ppermute | solution.py:17
  53.5 1.9 %collective-permute-done.6 = bf16[1,64,4,128]{3,1,2,0:T(8,128)(2,1)S(1)} collective-permute-done((bf16[1,64,4,128]{3,1,2,0:T(8,128)(2,1)S(1)}, bf16[1,64,4,128]{3,1,2,0:T(8,128)(2,1)S(1)}, u32[]{:S(2)}, u32[]{:S(2)}) %collective-permute-start.6) | collective-permute-done | bytes 65568 | tf_op jit(solution)/shard_map/ppermute | solution.py:14
  55.4 0.0 collective-permute-start.8
  55.4 0.0 collective-permute-done.7
  55.4 4.5 %collective-permute-start.9 = (bf16[1,64,4,128]{3,1,2,0:T(8,128)(2,1)S(1)}, bf16[1,64,4,128]{3,1,2,0:T(8,128)(2,1)S(1)}, u32[]{:S(2)}, u32[]{:S(2)}) collective-permute-start(bf16[1,64,4,128]{3,1,2,0:T(8,128)(2,1)S(1)} %collective-permute-done.7), channel_id=1, source_target_pairs={{0,15},{1,0},{2,1},{3,2},{4,3},{5,4},{6,5},{7,6},{8,7},{9,8},{10,9... | collective-permute-start | bytes 196616 | tf_op jit(solution)/shard_map/ppermute | solution.py:17
  59.9 1.8 %collective-permute-done.8 = bf16[1,64,4,128]{3,1,2,0:T(8,128)(2,1)S(1)} collective-permute-done((bf16[1,64,4,128]{3,1,2,0:T(8,128)(2,1)S(1)}, bf16[1,64,4,128]{3,1,2,0:T(8,128)(2,1)S(1)}, u32[]{:S(2)}, u32[]{:S(2)}) %collective-permute-start.8) | collective-permute-done | bytes 65568 | tf_op jit(solution)/shard_map/ppermute | solution.py:14
  61.8 0.0 collective-permute-start.10
  61.8 0.0 collective-permute-done.9
  61.8 4.5 %collective-permute-start.11 = (bf16[1,64,4,128]{3,1,2,0:T(8,128)(2,1)S(1)}, bf16[1,64,4,128]{3,1,2,0:T(8,128)(2,1)S(1)}, u32[]{:S(2)}, u32[]{:S(2)}) collective-permute-start(bf16[1,64,4,128]{3,1,2,0:T(8,128)(2,1)S(1)} %collective-permute-done.9), channel_id=1, source_target_pairs={{0,15},{1,0},{2,1},{3,2},{4,3},{5,4},{6,5},{7,6},{8,7},{9,8},{10,9... | collective-permute-start | bytes 196616 | tf_op jit(solution)/shard_map/ppermute | solution.py:17
  66.3 1.8 %collective-permute-done.10 = bf16[1,64,4,128]{3,1,2,0:T(8,128)(2,1)S(1)} collective-permute-done((bf16[1,64,4,128]{3,1,2,0:T(8,128)(2,1)S(1)}, bf16[1,64,4,128]{3,1,2,0:T(8,128)(2,1)S(1)}, u32[]{:S(2)}, u32[]{:S(2)}) %collective-permute-start.10) | collective-permute-done | bytes 65568 | tf_op jit(solution)/shard_map/ppermute | solution.py:14
  68.2 0.0 collective-permute-start.12
  68.2 0.0 collective-permute-done.11
  68.2 4.5 %collective-permute-start.13 = (bf16[1,64,4,128]{3,1,2,0:T(8,128)(2,1)S(1)}, bf16[1,64,4,128]{3,1,2,0:T(8,128)(2,1)S(1)}, u32[]{:S(2)}, u32[]{:S(2)}) collective-permute-start(bf16[1,64,4,128]{3,1,2,0:T(8,128)(2,1)S(1)} %collective-permute-done.11), channel_id=1, source_target_pairs={{0,15},{1,0},{2,1},{3,2},{4,3},{5,4},{6,5},{7,6},{8,7},{9,8},{10,9... | collective-permute-start | bytes 196616 | tf_op jit(solution)/shard_map/ppermute | solution.py:17
  72.7 1.8 %collective-permute-done.12 = bf16[1,64,4,128]{3,1,2,0:T(8,128)(2,1)S(1)} collective-permute-done((bf16[1,64,4,128]{3,1,2,0:T(8,128)(2,1)S(1)}, bf16[1,64,4,128]{3,1,2,0:T(8,128)(2,1)S(1)}, u32[]{:S(2)}, u32[]{:S(2)}) %collective-permute-start.12) | collective-permute-done | bytes 65568 | tf_op jit(solution)/shard_map/ppermute | solution.py:14
  74.6 0.0 collective-permute-start.14
  74.6 0.0 collective-permute-done.13
  74.6 6.3 %collective-permute-done.14 = bf16[1,64,4,128]{3,1,2,0:T(8,128)(2,1)S(1)} collective-permute-done((bf16[1,64,4,128]{3,1,2,0:T(8,128)(2,1)S(1)}, bf16[1,64,4,128]{3,1,2,0:T(8,128)(2,1)S(1)}, u32[]{:S(2)}, u32[]{:S(2)}) %collective-permute-start.14) | collective-permute-done | bytes 65568 | tf_op jit(solution)/shard_map/ppermute | solution.py:14
  81.0 2.1 %gather_fusion.1 = bf16[32,64,4,128]{3,1,2,0:T(8,128)(2,1)} fusion(bf16[16,64,4,128]{3,1,2,0:T(8,128)(2,1)S(1)} %constant_dynamic-update-slice_fusion, s32[1024]{0:T(1024)S(1)} %pad_clamp_fusion), kind=kCustom, calls=%fused_computation.1 | custom fusion | bytes 4194432 | tf_op jit(solution)/shard_map/gather | solution.py:73
  83.1 3.1 %copy.101 = bf16[32,64,4,128]{3,1,0,2:T(8,128)(2,1)} copy(bf16[32,64,4,128]{3,1,2,0:T(8,128)(2,1)} %gather_fusion.1) | data formatting | bytes 4194304 | tf_op jit(solution)/shard_map/gather | solution.py:73
  86.2 3.4 %gather_fusion = bf16[32,64,4,128]{3,1,2,0:T(8,128)(2,1)} fusion(bf16[16,64,4,128]{3,1,2,0:T(8,128)(2,1)} %all-gather.2.cloned.1.call-done, s32[1024]{0:T(1024)S(1)} %pad_clamp_fusion), kind=kCustom, calls=%fused_computation | custom fusion | bytes 4194432 | tf_op jit(solution)/shard_map/gather | solution.py:72
  89.6 1.8 %copy.94 = bf16[32,64,4,128]{3,1,0,2:T(8,128)(2,1)S(1)} copy(bf16[32,64,4,128]{3,1,2,0:T(8,128)(2,1)} %gather_fusion) | data formatting | bytes 4194304 | tf_op jit(solution)/shard_map/gather | solution.py:72
  91.5 0.0 copy-start.6
  91.5 0.9 bitcast_reduce_fusion
  92.5 0.1 fusion.33
  92.5 0.4 fusion.35
  92.9 0.2 copy-done.1
  93.1 1.6 %fusion.11 = (f32[8,4,64]{2,1,0:T(4,128)S(1)}, f32[8,4,64]{2,1,0:T(4,128)S(1)}) fusion(f32[8,4,64,256]{3,2,1,0:T(8,128)S(1)} %copy-done.1, f32[8,4,64]{2,1,0:T(4,128)S(1)} %bitcast.45, pred[8,256]{1,0:T(8,128)(4,1)S(1)} %iota_compare_fusion, f32[8,4,256,64]{2,3,1,0:T(8,128)S(1)} %get-tuple-element.10), kind=kLoop, calls=%fused_computation.17 | loop fusion | flops 3665920 | bytes 4220928 | tf_op jit(solution)/shard_map/reduce_sum | solution.py:83
  94.7 0.0 copy-done.4
  94.7 0.9 fusion.13
  95.6 0.6 copy-done.5
  96.3 0.9 fusion.22
  97.2 0.9 copy.103
  (31 shorter events, 0.3 us)
Async XLA Ops:
  6.5 25.2 %copy-start = (bf16[8,256,4,128]{3,2,1,0:T(4,128)(2,1)S(1)}, bf16[8,256,4,128]{3,2,1,0:T(4,128)(2,1)}, u32[]{:S(2)}) copy-start(bf16[8,256,4,128]{3,2,1,0:T(4,128)(2,1)} %param.13) | copy-start | bytes 6291460
  6.5 79.7 %all-gather.2.cloned.1.call-start = ((), (), s32[]{:S(2)}) async-start(), calls=%async_computation | async-start | bytes 1114112 | tf_op jit(solution)/shard_map/all_gather | solution.py:60
  7.8 27.7 %collective-permute-start = (bf16[1,64,4,128]{3,1,2,0:T(8,128)(2,1)S(1)}, bf16[1,64,4,128]{3,1,2,0:T(8,128)(2,1)S(1)}, u32[]{:S(2)}, u32[]{:S(2)}) collective-permute-start(bf16[1,64,4,128]{3,1,2,0:T(8,128)(2,1)S(1)} %get-tuple-element.7), channel_id=1, source_target_pairs={{0,1},{1,2},{2,3},{3,4},{4,5},{5,6},{6,7},{7,8},{8,9},{9,10},{10,1... | collective-permute-start | bytes 196616 | tf_op jit(solution)/shard_map/ppermute | solution.py:14
  8.3 27.2 %collective-permute-start.1 = (bf16[1,64,4,128]{3,1,2,0:T(8,128)(2,1)S(1)}, bf16[1,64,4,128]{3,1,2,0:T(8,128)(2,1)S(1)}, u32[]{:S(2)}, u32[]{:S(2)}) collective-permute-start(bf16[1,64,4,128]{3,1,2,0:T(8,128)(2,1)S(1)} %get-tuple-element.7), channel_id=1, source_target_pairs={{0,15},{1,0},{2,1},{3,2},{4,3},{5,4},{6,5},{7,6},{8,7},{9,8},{10,9... | collective-permute-start | bytes 196616 | tf_op jit(solution)/shard_map/ppermute | solution.py:17
  31.7 3.3 %copy-start.2 = (bf16[8,4,4,16,128]{4,3,2,1,0:T(8,128)(2,1)S(1)}, bf16[8,4,4,16,128]{4,3,2,1,0:T(8,128)(2,1)}, u32[]{:S(2)}) copy-start(bf16[8,4,4,16,128]{4,3,2,1,0:T(8,128)(2,1)} %copy.89) | copy-start | bytes 1572868
  31.7 3.3 %copy-start.7 = (bf16[8,4,4,128]{3,2,1,0:T(4,128)(2,1)S(1)}, bf16[8,4,4,128]{3,2,1,0:T(4,128)(2,1)}, u32[]{:S(2)}) copy-start(bf16[8,4,4,128]{3,2,1,0:T(4,128)(2,1)} %param.11) | copy-start | bytes 98308
  35.5 6.6 %collective-permute-start.2 = (bf16[1,64,4,128]{3,1,2,0:T(8,128)(2,1)S(1)}, bf16[1,64,4,128]{3,1,2,0:T(8,128)(2,1)S(1)}, u32[]{:S(2)}, u32[]{:S(2)}) collective-permute-start(bf16[1,64,4,128]{3,1,2,0:T(8,128)(2,1)S(1)} %collective-permute-done), channel_id=1, source_target_pairs={{0,1},{1,2},{2,3},{3,4},{4,5},{5,6},{6,7},{7,8},{8,9},{9,10},{10,1... | collective-permute-start | bytes 196616 | tf_op jit(solution)/shard_map/ppermute | solution.py:14
  35.5 6.6 %collective-permute-start.3 = (bf16[1,64,4,128]{3,1,2,0:T(8,128)(2,1)S(1)}, bf16[1,64,4,128]{3,1,2,0:T(8,128)(2,1)S(1)}, u32[]{:S(2)}, u32[]{:S(2)}) collective-permute-start(bf16[1,64,4,128]{3,1,2,0:T(8,128)(2,1)S(1)} %collective-permute-done.1), channel_id=1, source_target_pairs={{0,15},{1,0},{2,1},{3,2},{4,3},{5,4},{6,5},{7,6},{8,7},{9,8},{10,9... | collective-permute-start | bytes 196616 | tf_op jit(solution)/shard_map/ppermute | solution.py:17
  42.0 7.0 %collective-permute-start.4 = (bf16[1,64,4,128]{3,1,2,0:T(8,128)(2,1)S(1)}, bf16[1,64,4,128]{3,1,2,0:T(8,128)(2,1)S(1)}, u32[]{:S(2)}, u32[]{:S(2)}) collective-permute-start(bf16[1,64,4,128]{3,1,2,0:T(8,128)(2,1)S(1)} %collective-permute-done.2), channel_id=1, source_target_pairs={{0,1},{1,2},{2,3},{3,4},{4,5},{5,6},{6,7},{7,8},{8,9},{9,10},{10,1... | collective-permute-start | bytes 196616 | tf_op jit(solution)/shard_map/ppermute | solution.py:14
  42.1 6.9 %collective-permute-start.5 = (bf16[1,64,4,128]{3,1,2,0:T(8,128)(2,1)S(1)}, bf16[1,64,4,128]{3,1,2,0:T(8,128)(2,1)S(1)}, u32[]{:S(2)}, u32[]{:S(2)}) collective-permute-start(bf16[1,64,4,128]{3,1,2,0:T(8,128)(2,1)S(1)} %collective-permute-done.3), channel_id=1, source_target_pairs={{0,15},{1,0},{2,1},{3,2},{4,3},{5,4},{6,5},{7,6},{8,7},{9,8},{10,9... | collective-permute-start | bytes 196616 | tf_op jit(solution)/shard_map/ppermute | solution.py:17
  49.0 6.4 %collective-permute-start.6 = (bf16[1,64,4,128]{3,1,2,0:T(8,128)(2,1)S(1)}, bf16[1,64,4,128]{3,1,2,0:T(8,128)(2,1)S(1)}, u32[]{:S(2)}, u32[]{:S(2)}) collective-permute-start(bf16[1,64,4,128]{3,1,2,0:T(8,128)(2,1)S(1)} %collective-permute-done.4), channel_id=1, source_target_pairs={{0,1},{1,2},{2,3},{3,4},{4,5},{5,6},{6,7},{7,8},{8,9},{9,10},{10,1... | collective-permute-start | bytes 196616 | tf_op jit(solution)/shard_map/ppermute | solution.py:14
  49.0 6.4 %collective-permute-start.7 = (bf16[1,64,4,128]{3,1,2,0:T(8,128)(2,1)S(1)}, bf16[1,64,4,128]{3,1,2,0:T(8,128)(2,1)S(1)}, u32[]{:S(2)}, u32[]{:S(2)}) collective-permute-start(bf16[1,64,4,128]{3,1,2,0:T(8,128)(2,1)S(1)} %collective-permute-done.5), channel_id=1, source_target_pairs={{0,15},{1,0},{2,1},{3,2},{4,3},{5,4},{6,5},{7,6},{8,7},{9,8},{10,9... | collective-permute-start | bytes 196616 | tf_op jit(solution)/shard_map/ppermute | solution.py:17
  55.4 6.4 %collective-permute-start.8 = (bf16[1,64,4,128]{3,1,2,0:T(8,128)(2,1)S(1)}, bf16[1,64,4,128]{3,1,2,0:T(8,128)(2,1)S(1)}, u32[]{:S(2)}, u32[]{:S(2)}) collective-permute-start(bf16[1,64,4,128]{3,1,2,0:T(8,128)(2,1)S(1)} %collective-permute-done.6), channel_id=1, source_target_pairs={{0,1},{1,2},{2,3},{3,4},{4,5},{5,6},{6,7},{7,8},{8,9},{9,10},{10,1... | collective-permute-start | bytes 196616 | tf_op jit(solution)/shard_map/ppermute | solution.py:14
  55.4 6.4 %collective-permute-start.9 = (bf16[1,64,4,128]{3,1,2,0:T(8,128)(2,1)S(1)}, bf16[1,64,4,128]{3,1,2,0:T(8,128)(2,1)S(1)}, u32[]{:S(2)}, u32[]{:S(2)}) collective-permute-start(bf16[1,64,4,128]{3,1,2,0:T(8,128)(2,1)S(1)} %collective-permute-done.7), channel_id=1, source_target_pairs={{0,15},{1,0},{2,1},{3,2},{4,3},{5,4},{6,5},{7,6},{8,7},{9,8},{10,9... | collective-permute-start | bytes 196616 | tf_op jit(solution)/shard_map/ppermute | solution.py:17
  61.8 6.4 %collective-permute-start.10 = (bf16[1,64,4,128]{3,1,2,0:T(8,128)(2,1)S(1)}, bf16[1,64,4,128]{3,1,2,0:T(8,128)(2,1)S(1)}, u32[]{:S(2)}, u32[]{:S(2)}) collective-permute-start(bf16[1,64,4,128]{3,1,2,0:T(8,128)(2,1)S(1)} %collective-permute-done.8), channel_id=1, source_target_pairs={{0,1},{1,2},{2,3},{3,4},{4,5},{5,6},{6,7},{7,8},{8,9},{9,10},{10,1... | collective-permute-start | bytes 196616 | tf_op jit(solution)/shard_map/ppermute | solution.py:14
  61.8 6.4 %collective-permute-start.11 = (bf16[1,64,4,128]{3,1,2,0:T(8,128)(2,1)S(1)}, bf16[1,64,4,128]{3,1,2,0:T(8,128)(2,1)S(1)}, u32[]{:S(2)}, u32[]{:S(2)}) collective-permute-start(bf16[1,64,4,128]{3,1,2,0:T(8,128)(2,1)S(1)} %collective-permute-done.9), channel_id=1, source_target_pairs={{0,15},{1,0},{2,1},{3,2},{4,3},{5,4},{6,5},{7,6},{8,7},{9,8},{10,9... | collective-permute-start | bytes 196616 | tf_op jit(solution)/shard_map/ppermute | solution.py:17
  68.2 6.4 %collective-permute-start.12 = (bf16[1,64,4,128]{3,1,2,0:T(8,128)(2,1)S(1)}, bf16[1,64,4,128]{3,1,2,0:T(8,128)(2,1)S(1)}, u32[]{:S(2)}, u32[]{:S(2)}) collective-permute-start(bf16[1,64,4,128]{3,1,2,0:T(8,128)(2,1)S(1)} %collective-permute-done.10), channel_id=1, source_target_pairs={{0,1},{1,2},{2,3},{3,4},{4,5},{5,6},{6,7},{7,8},{8,9},{9,10},{10,1... | collective-permute-start | bytes 196616 | tf_op jit(solution)/shard_map/ppermute | solution.py:14
  68.2 6.4 %collective-permute-start.13 = (bf16[1,64,4,128]{3,1,2,0:T(8,128)(2,1)S(1)}, bf16[1,64,4,128]{3,1,2,0:T(8,128)(2,1)S(1)}, u32[]{:S(2)}, u32[]{:S(2)}) collective-permute-start(bf16[1,64,4,128]{3,1,2,0:T(8,128)(2,1)S(1)} %collective-permute-done.11), channel_id=1, source_target_pairs={{0,15},{1,0},{2,1},{3,2},{4,3},{5,4},{6,5},{7,6},{8,7},{9,8},{10,9... | collective-permute-start | bytes 196616 | tf_op jit(solution)/shard_map/ppermute | solution.py:17
  74.6 6.4 %collective-permute-start.14 = (bf16[1,64,4,128]{3,1,2,0:T(8,128)(2,1)S(1)}, bf16[1,64,4,128]{3,1,2,0:T(8,128)(2,1)S(1)}, u32[]{:S(2)}, u32[]{:S(2)}) collective-permute-start(bf16[1,64,4,128]{3,1,2,0:T(8,128)(2,1)S(1)} %collective-permute-done.12), channel_id=1, source_target_pairs={{0,1},{1,2},{2,3},{3,4},{4,5},{5,6},{6,7},{7,8},{8,9},{9,10},{10,1... | collective-permute-start | bytes 196616 | tf_op jit(solution)/shard_map/ppermute | solution.py:14
  89.6 1.9 %copy-start.3 = (bf16[8,4,4,16,128]{4,3,2,1,0:T(8,128)(2,1)S(1)}, bf16[8,4,4,16,128]{4,3,2,1,0:T(8,128)(2,1)}, u32[]{:S(2)}) copy-start(bf16[8,4,4,16,128]{4,3,2,1,0:T(8,128)(2,1)} %copy.89) | copy-start | bytes 1572868
  91.5 1.1 %copy-start.6 = (bf16[8,4,4,128]{3,2,1,0:T(4,128)(2,1)S(1)}, bf16[8,4,4,128]{3,2,1,0:T(4,128)(2,1)}, u32[]{:S(2)}) copy-start(bf16[8,4,4,128]{3,2,1,0:T(4,128)(2,1)} %param.12) | copy-start | bytes 98308
  91.5 1.6 %copy-start.1 = (f32[8,4,64,256]{3,2,1,0:T(8,128)S(1)}, f32[8,4,64,256]{3,2,1,0:T(8,128)}, u32[]{:S(2)}) copy-start(f32[8,4,64,256]{3,2,1,0:T(8,128)} %get-tuple-element.12) | copy-start | bytes 6291460
  93.1 1.6 %copy-start.4 = (bf16[8,256,4,128]{3,2,1,0:T(4,128)(2,1)S(1)}, bf16[8,256,4,128]{3,2,1,0:T(4,128)(2,1)}, u32[]{:S(2)}) copy-start(bf16[8,256,4,128]{3,2,1,0:T(4,128)(2,1)} %param.14) | copy-start | bytes 6291460
  94.7 1.6 %copy-start.5 = (bf16[32,64,4,128]{3,1,0,2:T(8,128)(2,1)S(1)}, bf16[32,64,4,128]{3,1,0,2:T(8,128)(2,1)}, u32[]{:S(2)}) copy-start(bf16[32,64,4,128]{3,1,0,2:T(8,128)(2,1)} %copy.101) | copy-start | bytes 6291460
Sparse Core Ops, SparseCore 0:
  15.0 36.9 all-gather.1
